TPU v7x, 32 devices: a whole 2x2x4 slice. The times are simulated.
32 devices in a mesh: frame: 16 (over z, y, x), head: 2 (over core).
Axes of the slice: x: 2, y: 2, z: 4, core: 2. Of those that a mesh axis runs over, the one named last changes fastest.
Arguments:
- residual: bfloat16 [2048, 5120], P('frame', 'head'), may hold values from -48 to 48
- query_proj: bfloat16 [2048, 3072], P('frame', 'head'), may hold values from -200 to 200
- key_proj: bfloat16 [2048, 3072], P('frame', 'head'), may hold values from -200 to 200
- value_proj: bfloat16 [2048, 3072], P('frame', 'head'), may hold values from -6 to 6
- q_gain: float32 [3072], P('head'), may hold values from 1 to 3
- k_gain: float32 [3072], P('head'), may hold values from 1 to 3
- time_embed: float32 [5120], P(('frame', 'head')), may hold values from -6 to 6
- time_proj: bfloat16 [5120, 3, 5120], P(('frame', 'head')), may hold values from -0.15625 to 0.15625
- mod_table: float32 [3, 5120], P(None, 'head'), may hold values from -3 to 3
- out_weight: bfloat16 [3072, 5120], P('head'), may hold values from -0.109375 to 0.109375
Outputs:
- hidden_out: bfloat16 [2048, 5120], P('frame', 'head')
- mlp_input: bfloat16 [2048, 5120], P('frame', 'head')
All inputs are finite; a program needn't handle non-finite values.
Results may differ from a plain program's by a relative error of at most 0.0071.
Values may be sent and summed in bfloat16 or wider, within the bound.
A program may use at most 128 MiB of HBM per device.

v0:
```python
import math

import jax
import jax.numpy as jnp
from jax import lax
from jax.sharding import PartitionSpec as P

D = 5120
HEADS = 24
HD = 128


def accumulate(carry, queries, keys_block, values_block):
    count = keys_block.shape[0]
    heads_here = queries.shape[1]
    keys_three = keys_block.reshape(count, heads_here, HD)
    values_three = values_block.reshape(count, heads_here, HD).astype(jnp.float32)
    scores = jnp.einsum("thd,shd->ths", queries, keys_three, preferred_element_type=jnp.float32) * (
        1.0 / math.sqrt(HD)
    )
    top_old, total_old, summed = carry
    top_new = jnp.maximum(top_old, jnp.max(scores, axis=2))
    weights = jnp.exp(scores - top_new[:, :, None])
    total_new = jnp.sum(weights, axis=2)
    summed_new = jnp.einsum("ths,shd->thd", weights, values_three, precision=lax.Precision.HIGHEST)
    return (top_new, total_new, summed_new)


def shards(
    residual,
    query_proj,
    key_proj,
    value_proj,
    q_gain,
    k_gain,
    time_embed,
    time_proj,
    mod_table,
    out_weight,
):
    emb = jax.nn.silu(time_embed)
    partial_mod = jnp.einsum(
        "r,rcd->cd", emb, time_proj.astype(jnp.float32), precision=lax.Precision.HIGHEST
    )
    width = mod_table.shape[1]
    summed_mod = lax.psum(partial_mod, ("frame", "head"))
    share = lax.dynamic_slice_in_dim(summed_mod, lax.axis_index("head") * width, width, 1)
    modulation = mod_table + share
    gate = modulation[0]
    shift = modulation[1]
    scale = modulation[2]
    tok_rows = query_proj.shape[0]
    heads_here = query_proj.shape[1] // HD
    query_wide = query_proj.astype(jnp.float32)
    key_wide = key_proj.astype(jnp.float32)
    total_q, total_k = lax.psum(
        (jnp.sum(query_wide * query_wide, axis=1), jnp.sum(key_wide * key_wide, axis=1)), "head"
    )
    query_rms = lax.rsqrt(total_q / (HEADS * HD) + 1e-06)
    key_rms = lax.rsqrt(total_k / (HEADS * HD) + 1e-06)
    queries = (
        (query_wide * query_rms[:, None] * q_gain)
        .astype(jnp.bfloat16)
        .reshape(tok_rows, heads_here, HD)
    )
    start_state = (
        jnp.full((tok_rows, heads_here), -1e30, jnp.float32),
        jnp.zeros((tok_rows, heads_here), jnp.float32),
        jnp.zeros((tok_rows, heads_here, HD), jnp.float32),
    )
    every_scale = lax.all_gather(key_rms, "frame", axis=0, tiled=True)
    keys_block = (
        lax.all_gather(key_proj, "frame", axis=0, tiled=True).astype(jnp.float32)
        * every_scale[:, None]
        * k_gain
    ).astype(jnp.bfloat16)
    top_final, total_final, summed_final = accumulate(
        start_state, queries, keys_block, lax.all_gather(value_proj, "frame", axis=0, tiled=True)
    )
    attn = (
        (summed_final / total_final[:, :, None])
        .astype(jnp.bfloat16)
        .reshape(tok_rows, heads_here * HD)
    )
    proj = (
        lax.psum_scatter(
            lax.dot_general(
                out_weight, attn, (((0,), (1,)), ((), ())), preferred_element_type=jnp.float32
            ).astype(jnp.bfloat16),
            "head",
            scatter_dimension=0,
            tiled=True,
        )
        .astype(jnp.float32)
        .T
    )
    hidden_out = (residual.astype(jnp.float32) + gate * proj).astype(jnp.bfloat16)
    hidden32 = lax.optimization_barrier(hidden_out).astype(jnp.float32)
    row_sum, row_squares = lax.psum(
        (jnp.sum(hidden32, axis=1), jnp.sum(hidden32 * hidden32, axis=1)), "head"
    )
    mean = row_sum[:, None] / D
    var = row_squares[:, None] / D - mean * mean
    mlp_input = ((hidden32 - mean) * lax.rsqrt(var + 1e-06) * (1.0 + scale) + shift).astype(
        jnp.bfloat16
    )
    return (hidden_out, mlp_input)


def solution(mesh):
    in_specs = (
        P("frame", "head"),
        P("frame", "head"),
        P("frame", "head"),
        P("frame", "head"),
        P("head"),
        P("head"),
        P(("frame", "head")),
        P(("frame", "head"), None, None),
        P(None, "head"),
        P("head", None),
    )
    out_specs = (P("frame", "head"), P("frame", "head"))
    return jax.shard_map(shards, mesh=mesh, in_specs=in_specs, out_specs=out_specs, check_vma=False)
```

profile of v0, /device:TPU:0, one launch (start us, length us, event | category | flops | bytes accessed | tf_op | source)
XLA Modules:
  0.0 312.0 jit_solution(16471371955343777573)
XLA Ops:
  7.2 0.0 all-gather.4.cloned.1.call-start
  7.2 1.9 copy.22
  9.1 0.0 all-gather.4.cloned.1.call-update
  9.1 0.0 all-gather.6.cloned.1.call-start
  9.2 0.7 all-gather.6.cloned.1.call-update
  9.9 0.0 reduce-scatter.2.cloned.1.call-start
  9.9 1.2 copy.23
  11.2 1.2 multiply_reduce_fusion
  12.3 0.2 fusion.22
  12.6 2.6 all-reduce.1
  15.2 42.8 %all-gather = f32[16,1,128]{2,1,0:T(1,128)S(1)} all-gather(f32[1,1,128]{2,1,0:T(1,128)S(1)} %rsqrt_bitcast_fusion), channel_id=1, replica_groups=mesh['frame'=16,'head'=2] {'frame'}, dimensions={0}, use_global_device_ids=true | all-gather | bytes 8704 | tf_op jit(solution)/shard_map/all_gather | solution.py:71
  58.0 1.0 fusion.24
  59.0 70.0 %all-gather.4.cloned.1.call-done = bf16[2048,1536]{0,1:T(8,128)(2,1)} async-done(((bf16[128,1536]{0,1:T(8,128)(2,1)}), bf16[2048,1536]{0,1:T(8,128)(2,1)}) %all-gather.4.cloned.1.call-update) | async-done | bytes 6291472 | tf_op jit(solution)/shard_map/all_gather | solution.py:73
  129.0 6.9 %multiply_convert_fusion = bf16[2048,1536]{0,1:T(8,128)(2,1)} fusion(bf16[2048,1536]{0,1:T(8,128)(2,1)} %all-gather.4.cloned.1.call-done, f32[1536]{0:T(1024)} %param.15, f32[2048]{0:T(1024)S(1)} %bitcast.49), kind=kLoop, calls=%fused_computation.3 | loop fusion | flops 12582912 | bytes 12597248 | tf_op jit(solution)/shard_map/convert_element_type | solution.py:76
  135.9 4.7 %bitcast_reduce_fusion = (f32[128,12]{0,1:T(8,128)S(1)}, f32[12,2048,128]{2,1,0:T(8,128)S(1)}) fusion(bf16[2048,12,128]{0,2,1:T(8,128)(2,1)} %bitcast.44, bf16[128,12,128]{0,2,1:T(8,128)(2,1)S(1)} %bitcast.46), kind=kOutput, calls=%fused_computation.1 | convolution fusion | flops 811596288 | bytes 19273728 | tf_op jit(solution)/shard_map/thd,shd->ths/dot_general | solution.py:18
  140.6 4.5 %copy-done = f32[12,2048,128]{2,1,0:T(8,128)} copy-done((f32[12,2048,128]{2,1,0:T(8,128)}, f32[12,2048,128]{2,1,0:T(8,128)S(1)}, u32[]{:S(2)}) %copy-start) | copy-done | bytes 12582936
  145.2 2.1 fusion.1
  147.3 76.2 %all-gather.6.cloned.1.call-done = bf16[2048,1536]{1,0:T(8,128)(2,1)} async-done(((bf16[128,1536]{1,0:T(8,128)(2,1)}), bf16[2048,1536]{1,0:T(8,128)(2,1)}) %all-gather.6.cloned.1.call-update) | async-done | bytes 6291472 | tf_op jit(solution)/shard_map/all_gather | solution.py:78
  223.4 8.7 %copy.26 = bf16[2048,1536]{0,1:T(8,128)(2,1)} copy(bf16[2048,1536]{1,0:T(8,128)(2,1)} %all-gather.6.cloned.1.call-done) | data formatting | bytes 12582912 | tf_op jit(solution)/shard_map/all_gather | solution.py:78
  232.1 14.6 %fusion.19 = bf16[128,12,128]{0,2,1:T(8,128)(2,1)S(1)} fusion(bf16[2048,12,128]{0,2,1:T(8,128)(2,1)} %bitcast.45, f32[12,2048,128]{2,1,0:T(8,128)} %copy-done, f32[128,12]{0,1:T(8,128)S(1)} %broadcast_maximum_fusion, f32[128,12]{0,1:T(8,128)S(1)} %fusion.1), kind=kOutput, calls=%fused_computation.24 | convolution fusion | flops 4838522880 | bytes 19279872 | tf_op jit(solution)/shard_map/ths,shd->thd/dot_general | solution.py:25
  246.8 0.0 copy-start.4
  246.8 8.8 %fusion.6 = bf16[5120,128]{0,1:T(8,128)(2,1)} fusion(bf16[128,1536]{0,1:T(8,128)(2,1)S(1)} %bitcast.47, bf16[1536,5120]{1,0:T(8,128)(2,1)} %param.19), kind=kOutput, calls=%fused_computation.9 | convolution fusion | flops 2013921280 | bytes 17432576 | tf_op jit(solution)/shard_map/dot_general | solution.py:87
  255.6 0.0 reduce-scatter.2.cloned.1.call-update
  255.7 4.7 %fusion.27 = f32[1,3,5120]{2,0,1:T(1,128)S(1)} fusion(f32[160,1,1]{0,1,2:T(1,128)S(1)} %bitcast.50, bf16[160,3,5120]{2,0,1:T(8,128)(2,1)} %param.17), kind=kOutput, calls=%fused_computation.42 | convolution fusion | flops 29491200 | bytes 4977280 | tf_op jit(solution)/shard_map/r,rcd->cd/dot_general | solution.py:42
  260.4 39.6 %psum.35 = f32[3,5120]{1,0:T(4,128)S(1)} all-reduce(f32[3,5120]{1,0:T(4,128)S(1)} %bitcast.48), channel_id=1, replica_groups=mesh['frame'=16,'head'=2] {'frame','head'}, use_global_device_ids=true, to_apply=%region_0.1 | all-reduce | flops 15360 | bytes 122880 | tf_op jit(solution)/shard_map/psum | solution.py:46
  300.0 0.1 fusion.25
  300.1 0.0 reduce-scatter.2.cloned.1.call-done
  300.1 1.3 fusion.12
  301.4 0.0 copy-start.1
  301.4 0.3 convert_reduce_fusion
  301.7 2.5 all-reduce
  304.2 1.3 fusion.10
  (14 shorter events, 0.1 us)
Async XLA Ops:
  7.2 121.9 %all-gather.4.cloned.1.call-start = ((), (), s32[]{:S(2)}) async-start(), calls=%async_computation.1 | async-start | bytes 6684672 | tf_op jit(solution)/shard_map/all_gather | solution.py:73
  9.1 214.3 %all-gather.6.cloned.1.call-start = ((), (), s32[]{:S(2)}) async-start(), calls=%async_computation.2 | async-start | bytes 6684672 | tf_op jit(solution)/shard_map/all_gather | solution.py:78
  9.9 290.2 %reduce-scatter.2.cloned.1.call-start = ((), (), s32[]{:S(2)}) async-start(), calls=%async_computation.3 | async-start | bytes 1966080 | tf_op jit(solution)/shard_map/reduce_scatter | solution.py:86
  140.6 4.6 %copy-start = (f32[12,2048,128]{2,1,0:T(8,128)}, f32[12,2048,128]{2,1,0:T(8,128)S(1)}, u32[]{:S(2)}) copy-start(f32[12,2048,128]{2,1,0:T(8,128)S(1)} %get-tuple-element.14) | copy-start | bytes 37748740
  246.8 8.9 %copy-start.4 = (f32[160]{0:T(256)S(1)}, f32[160]{0:T(256)}, u32[]{:S(2)}) copy-start(f32[160]{0:T(256)} %param.16) | copy-start | bytes 1924
  255.6 44.4 %copy-start.3 = (f32[3,2560]{1,0:T(4,128)S(1)}, f32[3,2560]{1,0:T(4,128)}, u32[]{:S(2)}) copy-start(f32[3,2560]{1,0:T(4,128)} %param.18) | copy-start | bytes 92164
  255.6 44.5 %copy-start.2 = (bf16[128,2560]{1,0:T(8,128)(2,1)S(1)}, bf16[128,2560]{1,0:T(8,128)(2,1)}, u32[]{:S(2)}) copy-start(bf16[128,2560]{1,0:T(8,128)(2,1)} %param.10) | copy-start | bytes 1966084
  301.4 4.1 %copy-start.1 = (bf16[128,2560]{1,0:T(8,128)(2,1)}, bf16[128,2560]{1,0:T(8,128)(2,1)S(1)}, u32[]{:S(2)}) copy-start(bf16[128,2560]{1,0:T(8,128)(2,1)S(1)} %fusion.12) | copy-start | bytes 1966084
Sparse Core Ops, SparseCore 0:
  11.2 117.7 all-gather.3
  131.8 91.5 all-gather.5
  255.7 7.1 reduce-scatter.1
where the time goes:
time: 313 us; the launch traced here: 312 us
  waiting for transfers between devices  147 us (47%)
  blocking collectives  87.5 us (28%)
  matrix products  32.8 us (10%)
  local copies, waits for them, and re-layouts  16.4 us (5%)
  other arithmetic  14.3 us (5%)
  between operations  13.9 us (4%)
    all_gather x1, waiting for transfers between devices, shards(): lax.all_gather(value_proj, 'frame', axis=0, tiled=True)  76.2 us
    all_gather x1, waiting for transfers between devices, shards(): lax.all_gather(key_proj, 'frame', axis=0, tiled=True).astype(jnp.float32)  70 us
    all_gather x1, blocking collectives, shards(): every_scale = lax.all_gather(key_rms, 'frame', axis=0, tiled=True)  42.8 us
    psum x1, blocking collectives, shards(): summed_mod = lax.psum(partial_mod, ('frame', 'head'))  39.6 us
    dot_general x1, matrix products, accumulate(): jnp.einsum('ths,shd->thd', weights, values_three, precision=lax.Precision...  14.6 us
    dot_general x1, matrix products, shards(): lax.dot_general(out_weight, attn, (((0,), (1,)), ((), ())), preferred_ele...  8.81 us
    all_gather x1, local copies, waits for them, and re-layouts, shards(): lax.all_gather(value_proj, 'frame', axis=0, tiled=True)  8.7 us
    unnamed x12, local copies, waits for them, and re-layouts  7.7 us
  transfers between devices with their start and end apart: 3, of which 2 were waited for; matrix products, arithmetic and copies ran while one was open for 7% of the time, Pallas kernels for 0%

commit v1 on v0

v1 whole, which is shorter than its diff:
```python
import math

import jax
import jax.numpy as jnp
from jax import lax
from jax.experimental import pallas as pl
from jax.experimental.pallas import tpu as pltpu
from jax.sharding import PartitionSpec as P

D = 5120
HEADS = 24
HD = 128


MESH = pl.DeviceIdType.MESH
PLANE = 4
LINE = 4
ORDER = ((0, 0), (0, 1), (1, 0), (3, 0), (2, 0), (1, 1), (3, 1), (2, 1))


def remote(src, dst, send, recv, device):
    return pltpu.make_async_remote_copy(
        src_ref=src, dst_ref=dst, send_sem=send, recv_sem=recv, device_id=device, device_id_type=MESH
    )


def attend_kernel(
    q_ref, k_ref, v_ref, part_ref, attn_ref, mod_ref,
    kbuf, vbuf, qbuf, obuf, arecv, mpart, macc, mline, mx, my,
    own_sem, zs, zr, xs, xr, ys, yr, dxs, dxr, dys, dyr, os, orr, ms, mr,
):
    frames = LINE * PLANE
    f = lax.axis_index("frame")
    hd = lax.axis_index("head")
    z = lax.div(f, PLANE)
    x = lax.rem(f, 2)
    y = lax.rem(lax.div(f, 2), 2)
    step_x = 1 - 2 * x
    step_y = 2 - 4 * y
    to_x = {"frame": f + step_x}
    to_y = {"frame": f + step_y}
    to_pair = {"head": 1 - hd}
    rows = q_ref.shape[0]
    half = rows // 2
    width = q_ref.shape[1] // LINE

    def later(d):
        return lax.rem(f + PLANE * d, frames)

    def earlier(d):
        return lax.rem(f + frames - PLANE * d, frames)

    def piece(ref, line):
        return ref.at[:, pl.ds(pl.multiple_of(line * width, 128), width)]

    barrier = pltpu.get_barrier_semaphore()
    for d in range(1, LINE):
        pl.semaphore_signal(barrier, inc=1, device_id={"frame": later(d)}, device_id_type=MESH)
    for peer in (to_x, to_y, to_pair):
        pl.semaphore_signal(barrier, inc=1, device_id=peer, device_id_type=MESH)
    pl.semaphore_wait(barrier, LINE + 2)

    sends = []
    pair = remote(part_ref.at[1 - hd], mpart, ms.at[0], mr.at[0], to_pair)
    pair.start()
    sends.append(pair)
    bufs = (kbuf, vbuf)
    own = []
    for i, (src, dst) in enumerate(
        ((k_ref, kbuf.at[f]), (v_ref, vbuf.at[f]), (q_ref, qbuf.at[z]))
    ):
        copy = pltpu.make_async_copy(piece(src, z), dst, own_sem.at[i])
        copy.start()
        own.append(copy)
    for i, src in enumerate((k_ref, v_ref, q_ref)):
        for d in (1, 3, 2):
            peer = later(d)
            dst = qbuf.at[z] if i == 2 else bufs[i].at[f]
            n = i * 3 + d - 1
            copy = remote(piece(src, lax.div(peer, PLANE)), dst, zs.at[n], zr.at[n], {"frame": peer})
            copy.start()
            sends.append(copy)

    def first(n):
        d, b = ORDER[n]
        at = earlier(d)
        block = bufs[b].at[at]
        if d == 0:
            own[b].wait()
        else:
            m = b * 3 + d - 1
            remote(block, block, zs.at[m], zr.at[m], {"frame": at}).wait_recv()
        for s, r, peer in ((xs, xr, to_x), (ys, yr, to_y)):
            copy = remote(block, block, s.at[n], r.at[n], peer)
            copy.start()
            sends.append(copy)

    def second(n):
        d, b = ORDER[n]
        at = earlier(d)
        block = bufs[b].at[at + step_x]
        remote(block, block, xs.at[n], xr.at[n], to_x).wait_recv()
        part = block.at[pl.ds(half, half)]
        copy = remote(part, part, dys.at[n], dyr.at[n], to_y)
        copy.start()
        sends.append(copy)
        block = bufs[b].at[at + step_y]
        remote(block, block, ys.at[n], yr.at[n], to_y).wait_recv()
        part = block.at[pl.ds(0, half)]
        copy = remote(part, part, dxs.at[n], dxr.at[n], to_x)
        copy.start()
        sends.append(copy)

    def third(n):
        d, b = ORDER[n]
        block = bufs[b].at[earlier(d) + step_x + step_y]
        part = block.at[pl.ds(0, half)]
        remote(part, part, dxs.at[n], dxr.at[n], to_x).wait_recv()
        part = block.at[pl.ds(half, half)]
        remote(part, part, dys.at[n], dyr.at[n], to_y).wait_recv()

    for n in range(len(ORDER)):
        first(n)
        if n >= 1:
            second(n - 1)
        if n == 0:
            pair.wait_recv()
            macc[0] = part_ref[hd] + mpart[...]
            for d in range(1, LINE):
                copy = remote(macc.at[0], mline.at[d - 1], ms.at[d], mr.at[d], {"frame": later(d)})
                copy.start()
                sends.append(copy)
        if n == 2:
            for d in range(1, LINE):
                remote(macc.at[0], mline.at[d - 1], ms.at[d], mr.at[d], {"frame": earlier(d)}).wait_recv()
            macc[1] = macc[0] + mline[0] + mline[1] + mline[2]
            copy = remote(macc.at[1], mx, ms.at[4], mr.at[4], to_x)
            copy.start()
            sends.append(copy)
        if n == 4:
            remote(macc.at[1], mx, ms.at[4], mr.at[4], to_x).wait_recv()
            macc[2] = macc[1] + mx[...]
            copy = remote(macc.at[2], my, ms.at[5], mr.at[5], to_y)
            copy.start()
            sends.append(copy)
    second(len(ORDER) - 1)
    remote(macc.at[2], my, ms.at[5], mr.at[5], to_y).wait_recv()
    mod_ref[...] = macc[2] + my[...]
    own[2].wait()
    for d in range(1, LINE):
        block = qbuf.at[lax.div(earlier(d), PLANE)]
        remote(block, block, zs.at[5 + d], zr.at[5 + d], {"frame": earlier(d)}).wait_recv()
    for n in range(len(ORDER)):
        third(n)

    for h in range(width // HD):
        cols = slice(h * HD, (h + 1) * HD)

        def block_of(i, carry):
            keys = kbuf[:, :, cols].reshape(frames * rows, HD)
            values = vbuf[:, :, cols].reshape(frames * rows, HD)
            scores = lax.dot_general(
                qbuf[i, :, cols], keys, (((1,), (1,)), ((), ())), preferred_element_type=jnp.float32
            ) * (1.0 / math.sqrt(HD))
            weights = jnp.exp(scores - jnp.max(scores, axis=1, keepdims=True))
            total = jnp.sum(weights, axis=1, keepdims=True)
            summed = jnp.dot(weights.astype(jnp.bfloat16), values, preferred_element_type=jnp.float32)
            obuf[i, :, cols] = (summed / total).astype(jnp.bfloat16)
            return carry

        lax.fori_loop(0, LINE, block_of, 0)
        for d in range(1, LINE):
            n = h * 3 + d - 1
            copy = remote(
                obuf.at[lax.div(later(d), PLANE), :, cols], arecv.at[z, :, cols],
                os.at[n], orr.at[n], {"frame": later(d)},
            )
            copy.start()
            sends.append(copy)
        arecv[z, :, cols] = obuf[z, :, cols]
    for h in range(width // HD):
        cols = slice(h * HD, (h + 1) * HD)
        for d in range(1, LINE):
            n = h * 3 + d - 1
            block = arecv.at[lax.div(earlier(d), PLANE), :, cols]
            remote(block, block, os.at[n], orr.at[n], {"frame": earlier(d)}).wait_recv()
    for j in range(LINE):
        attn_ref[:, j * width : (j + 1) * width] = arecv[j]
    for copy in sends:
        copy.wait_send()


def attend(queries, keys, values, part):
    rows, cols = queries.shape
    width = cols // LINE
    heads_sub = width // HD
    half_mod = part.shape[1:]
    bf, f32 = jnp.bfloat16, jnp.float32
    dma = pltpu.SemaphoreType.DMA
    spec = pl.BlockSpec(memory_space=pltpu.VMEM)
    blocks = LINE * PLANE
    count = len(ORDER)
    return pl.pallas_call(
        attend_kernel,
        out_shape=(jax.ShapeDtypeStruct((rows, cols), bf), jax.ShapeDtypeStruct(half_mod, f32)),
        in_specs=[spec] * 4,
        out_specs=(spec, spec),
        scratch_shapes=[
            pltpu.VMEM((blocks, rows, width), bf),
            pltpu.VMEM((blocks, rows, width), bf),
            pltpu.VMEM((LINE, rows, width), bf),
            pltpu.VMEM((LINE, rows, width), bf),
            pltpu.VMEM((LINE, rows, width), bf),
            pltpu.VMEM(half_mod, f32),
            pltpu.VMEM((3,) + half_mod, f32),
            pltpu.VMEM((LINE - 1,) + half_mod, f32),
            pltpu.VMEM(half_mod, f32),
            pltpu.VMEM(half_mod, f32),
            dma((3,)), dma((9,)), dma((9,)),
        ]
        + [dma((count,))] * 8
        + [dma((3 * heads_sub,))] * 2
        + [dma((6,))] * 2,
        compiler_params=pltpu.CompilerParams(
            collective_id=0, has_side_effects=True, vmem_limit_bytes=40 * 1024 * 1024
        ),
    )(queries, keys, values, part)


def accumulate(carry, queries, keys_block, values_block):
    count = keys_block.shape[0]
    heads_here = queries.shape[1]
    keys_three = keys_block.reshape(count, heads_here, HD)
    values_three = values_block.reshape(count, heads_here, HD).astype(jnp.float32)
    scores = jnp.einsum("thd,shd->ths", queries, keys_three, preferred_element_type=jnp.float32) * (
        1.0 / math.sqrt(HD)
    )
    top_old, total_old, summed = carry
    top_new = jnp.maximum(top_old, jnp.max(scores, axis=2))
    weights = jnp.exp(scores - top_new[:, :, None])
    total_new = jnp.sum(weights, axis=2)
    summed_new = jnp.einsum("ths,shd->thd", weights, values_three, precision=lax.Precision.HIGHEST)
    return (top_new, total_new, summed_new)


def shards(
    residual,
    query_proj,
    key_proj,
    value_proj,
    q_gain,
    k_gain,
    time_embed,
    time_proj,
    mod_table,
    out_weight,
):
    emb = jax.nn.silu(time_embed)
    partial_mod = jnp.einsum(
        "r,rcd->cd", emb, time_proj.astype(jnp.float32), precision=lax.Precision.HIGHEST
    )
    width = mod_table.shape[1]
    groups = lax.axis_size("head")
    place = lax.axis_index("head")
    tok_rows = query_proj.shape[0]
    heads_here = query_proj.shape[1] // HD
    query_wide = query_proj.astype(jnp.float32)
    key_wide = key_proj.astype(jnp.float32)
    total_q, total_k = lax.psum(
        (jnp.sum(query_wide * query_wide, axis=1), jnp.sum(key_wide * key_wide, axis=1)), "head"
    )
    query_rms = lax.rsqrt(total_q / (HEADS * HD) + 1e-06)
    key_rms = lax.rsqrt(total_k / (HEADS * HD) + 1e-06)
    queries = (query_wide * query_rms[:, None] * q_gain).astype(jnp.bfloat16)
    keys = (key_wide * key_rms[:, None] * k_gain).astype(jnp.bfloat16)
    fused = groups == 2 and lax.axis_size("frame") == LINE * PLANE and heads_here % LINE == 0
    if fused:
        part = partial_mod.reshape(3, groups, width).transpose(1, 0, 2)
        attn, share = attend(queries, keys, value_proj, part)
    else:
        summed_mod = lax.psum(partial_mod, ("frame", "head"))
        share = lax.dynamic_slice_in_dim(summed_mod, place * width, width, 1)
        start_state = (
            jnp.full((tok_rows, heads_here), -1e30, jnp.float32),
            jnp.zeros((tok_rows, heads_here), jnp.float32),
            jnp.zeros((tok_rows, heads_here, HD), jnp.float32),
        )
        top_final, total_final, summed_final = accumulate(
            start_state,
            queries.reshape(tok_rows, heads_here, HD),
            lax.all_gather(keys, "frame", axis=0, tiled=True),
            lax.all_gather(value_proj, "frame", axis=0, tiled=True),
        )
        attn = (
            (summed_final / total_final[:, :, None])
            .astype(jnp.bfloat16)
            .reshape(tok_rows, heads_here * HD)
        )
    modulation = mod_table + share
    gate = modulation[0]
    shift = modulation[1]
    scale = modulation[2]
    if fused:
        full = jnp.dot(attn, out_weight, preferred_element_type=jnp.float32)
        mine = lax.dynamic_slice_in_dim(full, place * width, width, 1)
        other = lax.dynamic_slice_in_dim(full, (1 - place) * width, width, 1).astype(jnp.bfloat16)
        proj = mine + lax.ppermute(other, "head", [(0, 1), (1, 0)]).astype(jnp.float32)
    else:
        proj = (
            lax.psum_scatter(
                lax.dot_general(
                    out_weight, attn, (((0,), (1,)), ((), ())), preferred_element_type=jnp.float32
                ).astype(jnp.bfloat16),
                "head",
                scatter_dimension=0,
                tiled=True,
            )
            .astype(jnp.float32)
            .T
        )
    hidden_out = (residual.astype(jnp.float32) + gate * proj).astype(jnp.bfloat16)
    hidden32 = lax.optimization_barrier(hidden_out).astype(jnp.float32)
    row_sum, row_squares = lax.psum(
        (jnp.sum(hidden32, axis=1), jnp.sum(hidden32 * hidden32, axis=1)), "head"
    )
    mean = row_sum[:, None] / D
    var = row_squares[:, None] / D - mean * mean
    mlp_input = ((hidden32 - mean) * lax.rsqrt(var + 1e-06) * (1.0 + scale) + shift).astype(
        jnp.bfloat16
    )
    return (hidden_out, mlp_input)


def solution(mesh):
    in_specs = (
        P("frame", "head"),
        P("frame", "head"),
        P("frame", "head"),
        P("frame", "head"),
        P("head"),
        P("head"),
        P(("frame", "head")),
        P(("frame", "head"), None, None),
        P(None, "head"),
        P("head", None),
    )
    out_specs = (P("frame", "head"), P("frame", "head"))
    return jax.shard_map(shards, mesh=mesh, in_specs=in_specs, out_specs=out_specs, check_vma=False)
```

time: 313 us -> 99.8 us (0.32)
  waiting for transfers between devices: 147 us -> 2.33 us
  blocking collectives: 87.5 us -> 5.22 us
  Pallas kernels: 0 us -> 71.5 us
  matrix products: 32.8 us -> 12.2 us
  local copies, waits for them, and re-layouts: 16.4 us -> 0.97 us
  between operations: 13.9 us -> 0.75 us
  other arithmetic: 14.3 us -> 6.55 us
    all_gather x2 -> x0, waiting for transfers between devices: 146 us -> none  [the longest x1 76.2 us: shards(): lax.all_gather(value_proj, 'frame', axis=0, tiled=True)]
    pallas_call x0 -> x1, Pallas kernels: none -> 71.5 us  [attend(): pl.pallas_call(attend_kernel, out_shape=(jax.ShapeDtypeStruct((rows, cols...]
    all_gather x1 -> x0, blocking collectives: 42.8 us -> none  [shards(): every_scale = lax.all_gather(key_rms, 'frame', axis=0, tiled=True)]
    psum x1 -> x0, blocking collectives: 39.6 us -> none  [shards(): summed_mod = lax.psum(partial_mod, ('frame', 'head'))]
    dot_general x3 -> x1, matrix products: 28.1 us -> 7.68 us  [shards(): full = jnp.dot(attn, out_weight, preferred_element_type=jnp.float32)]
    all_gather x1 -> x0, local copies, waits for them, and re-layouts: 8.7 us -> none  [shards(): lax.all_gather(value_proj, 'frame', axis=0, tiled=True)]
    unnamed x12 -> x14, local copies, waits for them, and re-layouts: 7.7 us -> 0.04 us
    convert_element_type x2, other arithmetic: 7.86 us -> 0.32 us  [the longest x1 0.16 us: shards(): queries = (query_wide * query_rms[:, None] * q_gain).astype(jnp.bfloat16)]
  transfers between devices with their start and end apart: 3 -> 1, of which waited for: 2 -> 1; matrix products, arithmetic and copies ran while one was open for 7% -> 0% of each run, Pallas kernels for 0% -> 0%
where the time goes in v1:
time: 99.8 us; the launch traced here: 99.5 us
  Pallas kernels  71.5 us (72%)
  matrix products  12.2 us (12%)
  other arithmetic  6.55 us (7%)
  blocking collectives  5.22 us (5%)
  waiting for transfers between devices  2.33 us (2%)
    pallas_call x1, Pallas kernels, attend(): pl.pallas_call(attend_kernel, out_shape=(jax.ShapeDtypeStruct((rows, cols...  71.5 us
    dot_general x1, matrix products, shards(): full = jnp.dot(attn, out_weight, preferred_element_type=jnp.float32)  7.68 us
    dot_general x1, matrix products, shards(): jnp.einsum('r,rcd->cd', emb, time_proj.astype(jnp.float32), precision=lax...  4.48 us
    psum x1, blocking collectives, shards(): lax.psum((jnp.sum(query_wide * query_wide, axis=1), jnp.sum(key_wide * ke...  2.76 us
    psum x1, blocking collectives, shards(): lax.psum((jnp.sum(hidden32, axis=1), jnp.sum(hidden32 * hidden32, axis=1)...  2.47 us
    ppermute x1, waiting for transfers between devices, shards(): lax.ppermute(other, 'head', [(0, 1), (1, 0)]).astype(jnp.float32)  2.33 us
  transfers between devices with their start and end apart: 1, of which 1 were waited for; matrix products, arithmetic and copies ran while one was open for 0% of the time, Pallas kernels for 0%

profile of v1, /device:TPU:0, one launch (start us, length us, event | category | flops | bytes accessed | tf_op | source)
XLA Modules:
  0.0 99.5 jit_solution(15044222751922673565)
XLA Ops:
  0.6 1.2 %fusion.5 = f32[128]{0:T(128)S(1)} fusion(bf16[128,1536]{1,0:T(8,128)(2,1)} %param.11), kind=kLoop, calls=%fused_computation.14 | loop fusion | flops 589696 | bytes 393728 | tf_op jit(solution)/shard_map/reduce_sum | solution.py:270
  1.8 1.2 %fusion.8 = f32[128]{0:T(128)S(1)} fusion(bf16[128,1536]{1,0:T(8,128)(2,1)} %param.12), kind=kLoop, calls=%fused_computation.17 | loop fusion | flops 589696 | bytes 393728 | tf_op jit(solution)/shard_map/reduce_sum | solution.py:270
  3.0 0.7 divide_multiply_fusion
  3.6 0.0 copy-start.2
  3.6 0.0 copy-start.5
  3.6 0.0 copy-start.3
  3.7 0.0 copy-start.6
  3.7 4.5 %fusion.12 = f32[1,3,5120]{2,0,1:T(1,128)S(1)} fusion(f32[160,1,1]{0,1,2:T(1,128)S(1)} %bitcast.11, bf16[160,3,5120]{2,0,1:T(8,128)(2,1)} %param.17), kind=kOutput, calls=%fused_computation.29 | convolution fusion | flops 29491200 | bytes 4977280 | tf_op jit(solution)/shard_map/r,rcd->cd/dot_general | solution.py:259
  8.1 0.0 copy-start
  8.2 2.8 %all-reduce.1 = (f32[128]{0:T(128)S(1)}, f32[128]{0:T(128)S(1)}) all-reduce(f32[128]{0:T(128)S(1)} %fusion.5, f32[128]{0:T(128)S(1)} %fusion.8), channel_id=1, replica_groups=mesh['frame'=16,'head'=2] {'head'}, use_global_device_ids=true, to_apply=%region_1.2 | all-reduce | flops 256 | bytes 2048 | tf_op jit(solution)/shard_map/psum | solution.py:269
  10.9 0.0 copy-done.2
  10.9 0.0 copy-done.5
  11.0 0.2 fusion.10.k_ref
  11.1 0.0 copy-done.3
  11.1 0.0 copy-done.6
  11.1 0.2 fusion.7.q_ref
  11.3 0.0 copy-done
  11.3 71.5 %shard_map.113 = (bf16[128,1536]{1,0:T(8,128)(2,1)S(1)}, f32[3,2560]{1,0:T(4,128)S(1)}) custom-call(bf16[128,1536]{1,0:T(8,128)(2,1)S(1)} %fusion.7.q_ref, bf16[128,1536]{1,0:T(8,128)(2,1)S(1)} %fusion.10.k_ref, bf16[128,1536]{1,0:T(8,128)(2,1)S(1)} %copy-done, f32[2,3,2560]{2,1,0:T(4,128)S(1)} %bitcast.10), custom_call_target="tpu_custom_call" | custom-call | tf_op jit(solution)/shard_map/pallas_call | solution.py:203
  82.9 7.7 %fusion.13 = f32[128,5120]{1,0:T(8,128)S(1)} fusion(bf16[128,1536]{1,0:T(8,128)(2,1)S(1)} %get-tuple-element.5, bf16[1536,5120]{1,0:T(8,128)(2,1)} %param.19), kind=kOutput, calls=%fused_computation.30 | convolution fusion | flops 2013265920 | bytes 18743296 | tf_op jit(solution)/shard_map/dot_general | solution.py:304
  90.5 0.0 copy-start.4
  90.6 0.9 dynamic-slice_convert_fusion
  91.5 0.0 collective-permute-start
  91.5 0.0 copy-done.4
  91.5 0.1 fusion.11
  91.6 2.3 %collective-permute-done = bf16[128,2560]{1,0:T(8,128)(2,1)} collective-permute-done((bf16[128,2560]{1,0:T(8,128)(2,1)}, bf16[128,2560]{1,0:T(8,128)(2,1)}, u32[]{:S(2)}, u32[]{:S(2)}) %collective-permute-start) | collective-permute-done | bytes 655392 | tf_op jit(solution)/shard_map/ppermute | solution.py:307
  93.9 1.5 %add_convert_fusion = bf16[128,2560]{1,0:T(8,128)(2,1)S(1)} fusion(bf16[128,2560]{1,0:T(8,128)(2,1)} %collective-permute-done, f32[128,5120]{1,0:T(8,128)S(1)} %fusion.13, s32[]{:T(128)S(6)} %select_n.6, bf16[128,2560]{1,0:T(8,128)(2,1)} %param.10, f32[2560]{0:T(1024)S(1)} %get-tuple-element.10), kind=kLoop, calls=%fused_computation.8 | loop fusion | flops 1966080 | bytes 3287044 | tf_op jit(solution)/shard_map/convert_element_type | solution.py:321
  95.4 0.0 copy-start.1
  95.5 0.3 convert_reduce_fusion
  95.7 2.5 %all-reduce = (f32[128]{0:T(128)S(1)}, f32[128]{0:T(128)S(1)}) all-reduce(f32[128]{0:T(128)S(1)} %get-tuple-element.7, f32[128]{0:T(128)S(1)} %get-tuple-element.6), channel_id=1, replica_groups=mesh['frame'=16,'head'=2] {'head'}, use_global_device_ids=true, to_apply=%region_7.8 | all-reduce | flops 256 | bytes 2048 | tf_op jit(solution)/shard_map/psum | solution.py:323
  98.2 1.3 %fusion.3 = bf16[128,2560]{1,0:T(8,128)(2,1)} fusion(bf16[128,2560]{1,0:T(8,128)(2,1)S(1)} %add_convert_fusion, f32[2560]{0:T(1024)S(1)} %get-tuple-element.9, f32[2560]{0:T(1024)S(1)} %get-tuple-element.8, f32[128]{0:T(128)S(1)} %get-tuple-element.16, f32[128]{0:T(128)S(1)} %get-tuple-element.15), kind=kLoop, calls=%fused_computation.6 | loop fusion | flops 1966080 | bytes 1332224 | tf_op jit(solution)/shard_map/convert_element_type | solution.py:328
  99.5 0.0 copy-done.1
  (4 shorter events, 0.1 us)
Async XLA Ops:
  3.6 7.3 %copy-start.2 = (bf16[128,1536]{1,0:T(8,128)(2,1)S(1)}, bf16[128,1536]{1,0:T(8,128)(2,1)}, u32[]{:S(2)}) copy-start(bf16[128,1536]{1,0:T(8,128)(2,1)} %param.12) | copy-start | bytes 1179652
  3.6 7.3 %copy-start.5 = (f32[1536]{0:T(1024)S(1)}, f32[1536]{0:T(1024)}, u32[]{:S(2)}) copy-start(f32[1536]{0:T(1024)} %param.15) | copy-start | bytes 18436
  3.6 7.5 %copy-start.3 = (bf16[128,1536]{1,0:T(8,128)(2,1)S(1)}, bf16[128,1536]{1,0:T(8,128)(2,1)}, u32[]{:S(2)}) copy-start(bf16[128,1536]{1,0:T(8,128)(2,1)} %param.11) | copy-start | bytes 1179652
  3.7 7.5 %copy-start.6 = (f32[1536]{0:T(1024)S(1)}, f32[1536]{0:T(1024)}, u32[]{:S(2)}) copy-start(f32[1536]{0:T(1024)} %param.14) | copy-start | bytes 18436
  8.1 3.2 %copy-start = (bf16[128,1536]{1,0:T(8,128)(2,1)S(1)}, bf16[128,1536]{1,0:T(8,128)(2,1)}, u32[]{:S(2)}) copy-start(bf16[128,1536]{1,0:T(8,128)(2,1)} %v_ref.1) | copy-start | bytes 1179652
  90.5 0.9 copy-start.4
  91.5 2.4 %collective-permute-start = (bf16[128,2560]{1,0:T(8,128)(2,1)}, bf16[128,2560]{1,0:T(8,128)(2,1)}, u32[]{:S(2)}, u32[]{:S(2)}) collective-permute-start(bf16[128,2560]{1,0:T(8,128)(2,1)} %dynamic-slice_convert_fusion), channel_id=1, source_target_pairs={{0,1},{1,0},{2,3},{3,2},{4,5},{5,4},{6,7},{7,6},{8,9},{9,8},{10,11... | collective-permute-start | bytes 1966088 | tf_op jit(solution)/shard_map/ppermute | solution.py:307
  95.4 4.1 %copy-start.1 = (bf16[128,2560]{1,0:T(8,128)(2,1)}, bf16[128,2560]{1,0:T(8,128)(2,1)S(1)}, u32[]{:S(2)}) copy-start(bf16[128,2560]{1,0:T(8,128)(2,1)S(1)} %add_convert_fusion) | copy-start | bytes 1966084

commit v2 on v0

--- a/solution.py
+++ b/solution.py
@@ -3,11 +3,367 @@
 import jax
 import jax.numpy as jnp
 from jax import lax
+from jax.experimental import pallas as pl
+from jax.experimental.pallas import tpu as pltpu
 from jax.sharding import PartitionSpec as P
 
 D = 5120
 HEADS = 24
 HD = 128
+
+
+MESH = pl.DeviceIdType.MESH
+PLANE = 4
+LINE = 4
+ORDER = ((0, 1), (0, 0), (1, 1), (3, 1), (2, 1), (1, 0), (3, 0), (2, 0))
+INDEX = {pair: n for n, pair in enumerate(ORDER)}
+TILE = 512
+WEIGHT_PARTS = 4
+
+
+def remote(src, dst, send, recv, device):
+    return pltpu.make_async_remote_copy(
+        src_ref=src, dst_ref=dst, send_sem=send, recv_sem=recv, device_id=device, device_id_type=MESH
+    )
+
+
+def block_kernel(
+    q_ref, k_ref, v_hbm, qg_ref, kg_ref, te_ref, table_ref, res_hbm, proj_hbm, weight_hbm,
+    hidden_ref, mlp_ref,
+    qn, kn, kbuf, vbuf, qbuf, obuf, arecv, attn, top, total, summed,
+    squares, squares_in, part, mpart, macc, mline, mx, my, tbuf, wbuf, rbuf, pout, pin, stat, stat_in,
+    own_sem, load_sem, zs, zr, xs, xr, ys, yr, dxs, dxr, dys, dyr, os, orr, ms, mr, ps, pr, ss, sr,
+):
+    f32, bf = jnp.float32, jnp.bfloat16
+    frames = LINE * PLANE
+    f = lax.axis_index("frame")
+    hd = lax.axis_index("head")
+    z = lax.div(f, PLANE)
+    x = lax.rem(f, 2)
+    y = lax.rem(lax.div(f, 2), 2)
+    step_x = 1 - 2 * x
+    step_y = 2 - 4 * y
+    to_x = {"frame": f + step_x}
+    to_y = {"frame": f + step_y}
+    to_pair = {"head": 1 - hd}
+    rows, cols_all = q_ref.shape
+    half = rows // 2
+    width = cols_all // LINE
+    heads_sub = width // HD
+    owned = hidden_ref.shape[1]
+
+    def later(d):
+        return lax.rem(f + PLANE * d, frames)
+
+    def earlier(d):
+        return lax.rem(f + frames - PLANE * d, frames)
+
+    def piece(ref, line):
+        return ref.at[:, pl.ds(pl.multiple_of(line * width, 128), width)]
+
+    sends = []
+
+    def send(src, dst, s, r, peer):
+        copy = remote(src, dst, s, r, peer)
+        copy.start()
+        sends.append(copy)
+
+    loads = [pltpu.make_async_copy(proj_hbm, tbuf, load_sem.at[0])]
+    depth = cols_all // WEIGHT_PARTS
+    for i in range(WEIGHT_PARTS):
+        at = pl.ds(i * depth, depth)
+        loads.append(pltpu.make_async_copy(weight_hbm.at[at], wbuf.at[at], load_sem.at[1 + i]))
+    loads.append(pltpu.make_async_copy(res_hbm, rbuf, load_sem.at[1 + WEIGHT_PARTS]))
+
+    barrier = pltpu.get_barrier_semaphore()
+    for d in range(1, LINE):
+        pl.semaphore_signal(barrier, inc=1, device_id={"frame": later(d)}, device_id_type=MESH)
+    for peer in (to_x, to_y, to_pair):
+        pl.semaphore_signal(barrier, inc=1, device_id=peer, device_id_type=MESH)
+
+    for i, ref in enumerate((q_ref, k_ref)):
+        lanes = jnp.zeros((rows, 128), f32)
+        for c in range(0, cols_all, 128):
+            wide = ref[:, c : c + 128].astype(f32)
+            lanes += wide * wide
+        squares[i] = lanes
+    pl.semaphore_wait(barrier, LINE + 2)
+
+    bufs = (kbuf, vbuf)
+    own_v = pltpu.make_async_copy(piece(v_hbm, z), vbuf.at[f], own_sem.at[1])
+    own_v.start()
+    send(squares, squares_in, ss.at[0], sr.at[0], to_pair)
+
+    def send_line(i, src, dst):
+        for d in (1, 3, 2):
+            peer = later(d)
+            n = i * 3 + d - 1
+            send(piece(src, lax.div(peer, PLANE)), dst, zs.at[n], zr.at[n], {"frame": peer})
+
+    send_line(1, v_hbm, vbuf.at[f])
+    for copy in loads:
+        copy.start()
+
+    remote(squares, squares_in, ss.at[0], sr.at[0], to_pair).wait_recv()
+    for i, (ref, gain, out) in enumerate(((q_ref, qg_ref, qn), (k_ref, kg_ref, kn))):
+        sums = jnp.sum(squares[i] + squares_in[i], axis=1, keepdims=True)
+        rms = lax.rsqrt(sums / (HEADS * HD) + 1e-06)
+        for c in range(0, cols_all, 128):
+            at = slice(c, c + 128)
+            out[:, at] = (ref[:, at].astype(f32) * rms * gain[:, at]).astype(bf)
+    send_line(2, qn, qbuf.at[z])
+    send_line(0, kn, kbuf.at[f])
+    own_q = pltpu.make_async_copy(piece(qn, z), qbuf.at[z], own_sem.at[2])
+    own_q.start()
+    own_k = pltpu.make_async_copy(piece(kn, z), kbuf.at[f], own_sem.at[0])
+    own_k.start()
+    own = (own_k, own_v)
+
+    def first(d, b):
+        n = INDEX[d, b]
+        at = earlier(d)
+        block = bufs[b].at[at]
+        if d == 0:
+            own[b].wait()
+        else:
+            m = b * 3 + d - 1
+            remote(block, block, zs.at[m], zr.at[m], {"frame": at}).wait_recv()
+        send(block, block, xs.at[n], xr.at[n], to_x)
+        send(block, block, ys.at[n], yr.at[n], to_y)
+
+    def second(d, b):
+        n = INDEX[d, b]
+        at = earlier(d)
+        block = bufs[b].at[at + step_x]
+        remote(block, block, xs.at[n], xr.at[n], to_x).wait_recv()
+        low = block.at[pl.ds(half, half)]
+        send(low, low, dys.at[n], dyr.at[n], to_y)
+        block = bufs[b].at[at + step_y]
+        remote(block, block, ys.at[n], yr.at[n], to_y).wait_recv()
+        high = block.at[pl.ds(0, half)]
+        send(high, high, dxs.at[n], dxr.at[n], to_x)
+
+    def third(d, b):
+        n = INDEX[d, b]
+        block = bufs[b].at[earlier(d) + step_x + step_y]
+        high = block.at[pl.ds(0, half)]
+        remote(high, high, dxs.at[n], dxr.at[n], to_x).wait_recv()
+        low = block.at[pl.ds(half, half)]
+        remote(low, low, dys.at[n], dyr.at[n], to_y).wait_recv()
+
+    def absorb(d, opening, closing):
+        base = pl.multiple_of(lax.div(earlier(d), PLANE) * PLANE, PLANE)
+        group = pl.ds(base, PLANE)
+        for h in range(heads_sub):
+            cols = slice(h * HD, (h + 1) * HD)
+
+            def block_of(i, carry):
+                keys = kbuf[group, :, cols].reshape(PLANE * rows, HD)
+                values = vbuf[group, :, cols].reshape(PLANE * rows, HD)
+                scores = lax.dot_general(
+                    qbuf[i, :, cols], keys, (((1,), (1,)), ((), ())), preferred_element_type=f32
+                ) * (1.0 / math.sqrt(HD))
+                peak = jnp.max(scores, axis=1, keepdims=True)
+                if not opening:
+                    old = top[h, i]
+                    peak = jnp.maximum(old, peak)
+                    fade = jnp.exp(old - peak)
+                weights = jnp.exp(scores - peak)
+                count = jnp.sum(weights, axis=1, keepdims=True)
+                mixed = jnp.dot(weights.astype(bf), values, preferred_element_type=f32)
+                if not opening:
+                    count = count + fade * total[h, i]
+                    mixed = mixed + fade * summed[h, i]
+                if closing:
+                    obuf[i, :, cols] = (mixed / count).astype(bf)
+                else:
+                    top[h, i] = peak
+                    total[h, i] = count
+                    summed[h, i] = mixed
+                return carry
+
+            lax.fori_loop(0, LINE, block_of, 0)
+            if closing:
+                for e in range(1, LINE):
+                    n = h * 3 + e - 1
+                    send(
+                        obuf.at[lax.div(later(e), PLANE), :, cols], arecv.at[z, :, cols],
+                        os.at[n], orr.at[n], {"frame": later(e)},
+                    )
+                arecv[z, :, cols] = obuf[z, :, cols]
+
+    first(0, 1)
+    first(0, 0)
+    second(0, 1)
+    loads[0].wait()
+    t = te_ref[...]
+    emb = t / (1.0 + jnp.exp(-t))
+    high = emb.astype(bf).astype(f32)
+    middle = (emb - high).astype(bf).astype(f32)
+    low = emb - high - middle
+    row = lax.broadcasted_iota(jnp.int32, (8, emb.shape[1]), 0)
+    split = jnp.where(row == 0, high, jnp.where(row == 1, middle, jnp.where(row == 2, low, 0.0)))
+    split = split.astype(bf)
+    for c in range(3):
+        for side in range(2):
+            term = jnp.dot(
+                split, tbuf[c, :, side * owned : (side + 1) * owned], preferred_element_type=f32
+            )
+            part[side, c : c + 1, :] = jnp.sum(term, axis=0, keepdims=True)
+    send(part.at[1 - hd], mpart, ms.at[0], mr.at[0], to_pair)
+    second(0, 0)
+    first(1, 1)
+    first(3, 1)
+    remote(part.at[1 - hd], mpart, ms.at[0], mr.at[0], to_pair).wait_recv()
+    macc[0] = part[hd] + mpart[...]
+    for d in range(1, LINE):
+        send(macc.at[0], mline.at[d - 1], ms.at[d], mr.at[d], {"frame": later(d)})
+    second(1, 1)
+    first(2, 1)
+    second(3, 1)
+    own_q.wait()
+    for d in range(1, LINE):
+        block = qbuf.at[lax.div(earlier(d), PLANE)]
+        remote(block, block, zs.at[5 + d], zr.at[5 + d], {"frame": earlier(d)}).wait_recv()
+    second(2, 1)
+    third(0, 1)
+    third(0, 0)
+    absorb(0, True, False)
+    first(1, 0)
+    first(3, 0)
+    second(1, 0)
+    for d in range(1, LINE):
+        remote(macc.at[0], mline.at[d - 1], ms.at[d], mr.at[d], {"frame": earlier(d)}).wait_recv()
+    macc[1] = macc[0] + mline[0] + mline[1] + mline[2]
+    send(macc.at[1], mx, ms.at[4], mr.at[4], to_x)
+    first(2, 0)
+    second(3, 0)
+    third(1, 1)
+    third(1, 0)
+    absorb(1, False, False)
+    second(2, 0)
+    remote(macc.at[1], mx, ms.at[4], mr.at[4], to_x).wait_recv()
+    macc[2] = macc[1] + mx[...]
+    send(macc.at[2], my, ms.at[5], mr.at[5], to_y)
+    third(3, 1)
+    third(3, 0)
+    absorb(3, False, False)
+    third(2, 1)
+    third(2, 0)
+    absorb(2, False, True)
+
+    remote(macc.at[2], my, ms.at[5], mr.at[5], to_y).wait_recv()
+    macc[3] = macc[2] + my[...] + table_ref[...]
+    for copy in loads[1:]:
+        copy.wait()
+    for h in range(heads_sub):
+        cols = slice(h * HD, (h + 1) * HD)
+        for d in range(1, LINE):
+            n = h * 3 + d - 1
+            block = arecv.at[lax.div(earlier(d), PLANE), :, cols]
+            remote(block, block, os.at[n], orr.at[n], {"frame": earlier(d)}).wait_recv()
+    for j in range(LINE):
+        attn[:, j * width : (j + 1) * width] = arecv[j]
+
+    def project(side, at):
+        begin = pl.multiple_of(side * owned + at, 128)
+        return jnp.dot(attn[...], wbuf[:, pl.ds(begin, TILE)], preferred_element_type=f32)
+
+    for i in range(owned // TILE):
+        at = slice(i * TILE, (i + 1) * TILE)
+        pout[:, at] = project(1 - hd, i * TILE).astype(bf)
+        send(pout.at[:, at], pin.at[:, at], ps.at[i], pr.at[i], to_pair)
+    sum_lanes = jnp.zeros((rows, 128), f32)
+    square_lanes = jnp.zeros((rows, 128), f32)
+    for i in range(owned // TILE):
+        at = slice(i * TILE, (i + 1) * TILE)
+        mine = project(hd, i * TILE)
+        remote(pout.at[:, at], pin.at[:, at], ps.at[i], pr.at[i], to_pair).wait_recv()
+        mine = mine + pin[:, at].astype(f32)
+        hidden = (rbuf[:, at].astype(f32) + macc[3, 0:1, at] * mine).astype(bf)
+        hidden_ref[:, at] = hidden
+        wide = hidden.astype(f32)
+        for c in range(0, TILE, 128):
+            lane = wide[:, c : c + 128]
+            sum_lanes += lane
+            square_lanes += lane * lane
+    stat[0] = sum_lanes
+    stat[1] = square_lanes
+    send(stat, stat_in, ss.at[1], sr.at[1], to_pair)
+    remote(stat, stat_in, ss.at[1], sr.at[1], to_pair).wait_recv()
+    mean = jnp.sum(stat[0] + stat_in[0], axis=1, keepdims=True) / D
+    var = jnp.sum(stat[1] + stat_in[1], axis=1, keepdims=True) / D - mean * mean
+    spread = lax.rsqrt(var + 1e-06)
+    for i in range(owned // TILE):
+        at = slice(i * TILE, (i + 1) * TILE)
+        wide = hidden_ref[:, at].astype(f32)
+        mlp_ref[:, at] = (
+            (wide - mean) * spread * (1.0 + macc[3, 2:3, at]) + macc[3, 1:2, at]
+        ).astype(bf)
+    for copy in sends:
+        copy.wait_send()
+
+
+def fused_block(
+    residual, query_proj, key_proj, value_proj, q_gain, k_gain, time_embed, time_proj, mod_table, out_weight
+):
+    rows, cols = query_proj.shape
+    width = cols // LINE
+    heads_sub = width // HD
+    owned = residual.shape[1]
+    half_mod = mod_table.shape
+    bf, f32 = jnp.bfloat16, jnp.float32
+    dma = pltpu.SemaphoreType.DMA
+    vmem = pl.BlockSpec(memory_space=pltpu.VMEM)
+    hbm = pl.BlockSpec(memory_space=pl.ANY)
+    blocks = LINE * PLANE
+    count = len(ORDER)
+    lines = time_proj.transpose(1, 0, 2)
+    out = jax.ShapeDtypeStruct((rows, owned), bf)
+    slab = pltpu.VMEM((LINE, rows, width), bf)
+    lanes = pltpu.VMEM((2, rows, 128), f32)
+    column = pltpu.VMEM((heads_sub, LINE, rows, 1), f32)
+    return pl.pallas_call(
+        block_kernel,
+        out_shape=(out, out),
+        in_specs=[vmem, vmem, hbm, vmem, vmem, vmem, vmem, hbm, hbm, hbm],
+        out_specs=(vmem, vmem),
+        scratch_shapes=[
+            pltpu.VMEM((rows, cols), bf),
+            pltpu.VMEM((rows, cols), bf),
+            pltpu.VMEM((blocks, rows, width), bf),
+            pltpu.VMEM((blocks, rows, width), bf),
+            slab, slab, slab,
+            pltpu.VMEM((rows, cols), bf),
+            column, column,
+            pltpu.VMEM((heads_sub, LINE, rows, HD), f32),
+            lanes, lanes,
+            pltpu.VMEM((2,) + half_mod, f32),
+            pltpu.VMEM(half_mod, f32),
+            pltpu.VMEM((4,) + half_mod, f32),
+            pltpu.VMEM((LINE - 1,) + half_mod, f32),
+            pltpu.VMEM(half_mod, f32),
+            pltpu.VMEM(half_mod, f32),
+            pltpu.VMEM(lines.shape, bf),
+            pltpu.VMEM(out_weight.shape, bf),
+            pltpu.VMEM((rows, owned), bf),
+            pltpu.VMEM((rows, owned), bf),
+            pltpu.VMEM((rows, owned), bf),
+            lanes, lanes,
+            dma((3,)), dma((2 + WEIGHT_PARTS,)), dma((9,)), dma((9,)),
+        ]
+        + [dma((count,))] * 8
+        + [dma((3 * heads_sub,))] * 2
+        + [dma((6,))] * 2
+        + [dma((owned // TILE,))] * 2
+        + [dma((2,))] * 2,
+        compiler_params=pltpu.CompilerParams(
+            collective_id=0, has_side_effects=True, vmem_limit_bytes=60 * 1024 * 1024
+        ),
+    )(
+        query_proj, key_proj, value_proj, q_gain.reshape(1, cols), k_gain.reshape(1, cols),
+        time_embed.reshape(1, -1), mod_table, residual, lines, out_weight,
+    )
 
 
 def accumulate(carry, queries, keys_block, values_block):
@@ -38,6 +394,14 @@
     mod_table,
     out_weight,
 ):
+    if (
+        lax.axis_size("head") == 2
+        and lax.axis_size("frame") == LINE * PLANE
+        and query_proj.shape[1] % (LINE * HD) == 0
+    ):
+        return fused_block(
+            residual, query_proj, key_proj, value_proj, q_gain, k_gain, time_embed, time_proj, mod_table, out_weight
+        )
     emb = jax.nn.silu(time_embed)
     partial_mod = jnp.einsum(
         "r,rcd->cd", emb, time_proj.astype(jnp.float32), precision=lax.Precision.HIGHEST

time: 313 us -> 82.7 us (0.26)
  waiting for transfers between devices: 147 us -> 0 us
  blocking collectives: 87.5 us -> 0 us
  Pallas kernels: 0 us -> 74.8 us
  matrix products: 32.8 us -> 0 us
  other arithmetic: 14.3 us -> 0 us
  between operations: 13.9 us -> 0.64 us
  local copies, waits for them, and re-layouts: 16.4 us -> 6.52 us
    all_gather x2 -> x0, waiting for transfers between devices: 146 us -> none  [the longest x1 76.2 us: shards(): lax.all_gather(value_proj, 'frame', axis=0, tiled=True)]
    pallas_call x0 -> x1, Pallas kernels: none -> 74.8 us  [fused_block(): pl.pallas_call(block_kernel, out_shape=(out, out), in_specs=[vmem, vmem,...]
    psum x3 -> x0, blocking collectives: 44.7 us -> none  [the longest x1 39.6 us: shards(): summed_mod = lax.psum(partial_mod, ('frame', 'head'))]
    all_gather x1 -> x0, blocking collectives: 42.8 us -> none  [shards(): every_scale = lax.all_gather(key_rms, 'frame', axis=0, tiled=True)]
    dot_general x4 -> x0, matrix products: 32.8 us -> none  [the longest x1 14.6 us: accumulate(): jnp.einsum('ths,shd->thd', weights, values_three, precision=lax.Precision...]
    convert_element_type x4 -> x0, other arithmetic: 10.5 us -> none  [the longest x1 6.89 us: shards(): keys_block = (lax.all_gather(key_proj, 'frame', axis=0, tiled=True).astyp...]
    all_gather x1 -> x0, local copies, waits for them, and re-layouts: 8.7 us -> none  [shards(): lax.all_gather(value_proj, 'frame', axis=0, tiled=True)]
    unnamed x12 -> x2, local copies, waits for them, and re-layouts: 7.7 us -> 3.93 us
  transfers between devices with their start and end apart: 3 -> 0, of which waited for: 2 -> 0; matrix products, arithmetic and copies ran while one was open for 7% -> 0% of each run, Pallas kernels for 0% -> 0%
where the time goes in v2:
time: 82.7 us; the launch traced here: 82 us
  Pallas kernels  74.8 us (90%)
  local copies, waits for them, and re-layouts  6.52 us (8%)
    pallas_call x1, Pallas kernels, fused_block(): pl.pallas_call(block_kernel, out_shape=(out, out), in_specs=[vmem, vmem,...  74.8 us
    unnamed x2, local copies, waits for them, and re-layouts  3.93 us

profile of v2, /device:TPU:0, one launch (start us, length us, event | category | flops | bytes accessed | tf_op | source)
XLA Modules:
  0.0 82.0 jit_solution(18411390434233229678)
XLA Ops:
  0.6 1.3 %reshape.13.qg_ref = f32[1,1536]{1,0:T(1,128)} reshape(f32[1536]{0:T(1024)} %param.14) | data formatting | bytes 12288 | tf_op jit(solution)/shard_map/reshape | solution.py:364
  1.9 1.3 %reshape.14.kg_ref = f32[1,1536]{1,0:T(1,128)} reshape(f32[1536]{0:T(1024)} %param.15) | data formatting | bytes 12288 | tf_op jit(solution)/shard_map/reshape | solution.py:364
  3.2 74.8 %shard_map.113 = (bf16[128,2560]{1,0:T(8,128)(2,1)}, bf16[128,2560]{1,0:T(8,128)(2,1)}) custom-call(bf16[128,1536]{1,0:T(8,128)(2,1)} %q_ref.1, bf16[128,1536]{1,0:T(8,128)(2,1)} %k_ref.1, bf16[128,1536]{1,0:T(8,128)(2,1)} %v_hbm.1, f32[1,1536]{1,0:T(1,128)} %reshape.13.qg_ref, f32[1,1536]{1,0:T(1,128)} %reshape.14.kg_ref, f32[1,160]{1,0:T(1,128)} %bitcast.3, ...), custom_call_target="tpu_custom_call" | custom-call | tf_op jit(solution)/shard_map/pallas_call | solution.py:326
  78.1 2.0 %copy.14 = bf16[128,2560]{1,0:T(8,128)(2,1)} copy(bf16[128,2560]{1,0:T(8,128)(2,1)} %get-tuple-element.4) | data formatting | bytes 1310720
  80.0 2.0 %copy.15 = bf16[128,2560]{1,0:T(8,128)(2,1)} copy(bf16[128,2560]{1,0:T(8,128)(2,1)} %get-tuple-element.5) | data formatting | bytes 1310720

commit v3 on v2

--- a/solution.py
+++ b/solution.py
@@ -29,7 +29,7 @@
 
 def block_kernel(
     q_ref, k_ref, v_hbm, qg_ref, kg_ref, te_ref, table_ref, res_hbm, proj_hbm, weight_hbm,
-    hidden_ref, mlp_ref,
+    hidden_ref, row_ref, mod_ref,
     qn, kn, kbuf, vbuf, qbuf, obuf, arecv, attn, top, total, summed,
     squares, squares_in, part, mpart, macc, mline, mx, my, tbuf, wbuf, rbuf, pout, pin, stat, stat_in,
     own_sem, load_sem, zs, zr, xs, xr, ys, yr, dxs, dxr, dys, dyr, os, orr, ms, mr, ps, pr, ss, sr,
@@ -110,7 +110,7 @@
         rms = lax.rsqrt(sums / (HEADS * HD) + 1e-06)
         for c in range(0, cols_all, 128):
             at = slice(c, c + 128)
-            out[:, at] = (ref[:, at].astype(f32) * rms * gain[:, at]).astype(bf)
+            out[:, at] = (ref[:, at].astype(f32) * rms * gain[at].reshape(1, 128)).astype(bf)
     send_line(2, qn, qbuf.at[z])
     send_line(0, kn, kbuf.at[f])
     own_q = pltpu.make_async_copy(piece(qn, z), qbuf.at[z], own_sem.at[2])
@@ -182,7 +182,7 @@
                     summed[h, i] = mixed
                 return carry
 
-            lax.fori_loop(0, LINE, block_of, 0)
+            lax.fori_loop(0, LINE, block_of, 0, unroll=True)
             if closing:
                 for e in range(1, LINE):
                     n = h * 3 + e - 1
@@ -293,15 +293,20 @@
     remote(stat, stat_in, ss.at[1], sr.at[1], to_pair).wait_recv()
     mean = jnp.sum(stat[0] + stat_in[0], axis=1, keepdims=True) / D
     var = jnp.sum(stat[1] + stat_in[1], axis=1, keepdims=True) / D - mean * mean
-    spread = lax.rsqrt(var + 1e-06)
-    for i in range(owned // TILE):
-        at = slice(i * TILE, (i + 1) * TILE)
-        wide = hidden_ref[:, at].astype(f32)
-        mlp_ref[:, at] = (
-            (wide - mean) * spread * (1.0 + macc[3, 2:3, at]) + macc[3, 1:2, at]
-        ).astype(bf)
+    row_ref[0] = jnp.broadcast_to(mean, (rows, 128))
+    row_ref[1] = jnp.broadcast_to(lax.rsqrt(var + 1e-06), (rows, 128))
+    mod_ref[...] = macc[3]
     for copy in sends:
         copy.wait_send()
+
+
+def finish_kernel(hidden_ref, row_ref, mod_ref, hidden_out, mlp_out):
+    hidden = hidden_ref[...]
+    hidden_out[...] = hidden
+    wide = hidden.astype(jnp.float32)
+    mlp_out[...] = (
+        (wide - row_ref[0, :, 0:1]) * row_ref[1, :, 0:1] * (1.0 + mod_ref[2:3, :]) + mod_ref[1:2, :]
+    ).astype(jnp.bfloat16)
 
 
 def fused_block(
@@ -323,11 +328,11 @@
     slab = pltpu.VMEM((LINE, rows, width), bf)
     lanes = pltpu.VMEM((2, rows, 128), f32)
     column = pltpu.VMEM((heads_sub, LINE, rows, 1), f32)
-    return pl.pallas_call(
+    hidden, row, mod = pl.pallas_call(
         block_kernel,
-        out_shape=(out, out),
+        out_shape=(out, jax.ShapeDtypeStruct((2, rows, 128), f32), jax.ShapeDtypeStruct(half_mod, f32)),
         in_specs=[vmem, vmem, hbm, vmem, vmem, vmem, vmem, hbm, hbm, hbm],
-        out_specs=(vmem, vmem),
+        out_specs=(vmem, vmem, vmem),
         scratch_shapes=[
             pltpu.VMEM((rows, cols), bf),
             pltpu.VMEM((rows, cols), bf),
@@ -361,9 +366,22 @@
             collective_id=0, has_side_effects=True, vmem_limit_bytes=60 * 1024 * 1024
         ),
     )(
-        query_proj, key_proj, value_proj, q_gain.reshape(1, cols), k_gain.reshape(1, cols),
+        query_proj, key_proj, value_proj, q_gain, k_gain,
         time_embed.reshape(1, -1), mod_table, residual, lines, out_weight,
     )
+    tile = pl.BlockSpec((rows, TILE), lambda i: (0, i))
+    return pl.pallas_call(
+        finish_kernel,
+        out_shape=(out, out),
+        grid=(owned // TILE,),
+        in_specs=[
+            tile,
+            pl.BlockSpec((2, rows, 128), lambda i: (0, 0, 0)),
+            pl.BlockSpec((half_mod[0], TILE), lambda i: (0, i)),
+        ],
+        out_specs=(tile, tile),
+        compiler_params=pltpu.CompilerParams(vmem_limit_bytes=60 * 1024 * 1024),
+    )(hidden, row, mod)
 
 
 def accumulate(carry, queries, keys_block, values_block):

time: 82.7 us -> 74 us (0.89)
  local copies, waits for them, and re-layouts: 6.52 us -> 0 us
  Pallas kernels: 74.8 us -> 73.1 us
    unnamed x2 -> x0, local copies, waits for them, and re-layouts: 3.93 us -> none
    reshape x2 -> x0, local copies, waits for them, and re-layouts: 2.59 us -> none  [the longest x1 1.3 us: fused_block(): q_gain.reshape(1, cols)]
    pallas_call x1 -> x2, Pallas kernels: 74.8 us -> 73.1 us  [the longest x1 69 us: fused_block(): pl.pallas_call(block_kernel, out_shape=(out, jax.ShapeDtypeStruct((2, row...]
where the time goes in v3:
time: 74 us; the launch traced here: 73.7 us
  Pallas kernels  73.1 us (99%)
    pallas_call x1, Pallas kernels, fused_block(): pl.pallas_call(block_kernel, out_shape=(out, jax.ShapeDtypeStruct((2, row...  69 us
    pallas_call x1, Pallas kernels, fused_block(): pl.pallas_call(finish_kernel, out_shape=(out, out), grid=(owned // TILE,)...  4.05 us

profile of v3, /device:TPU:0, one launch (start us, length us, event | category | flops | bytes accessed | tf_op | source)
XLA Modules:
  0.0 73.7 jit_solution(12576849411491994370)
XLA Ops:
  0.6 69.0 %shard_map.113 = (bf16[128,2560]{1,0:T(8,128)(2,1)}, f32[2,128,128]{2,1,0:T(8,128)}, f32[3,2560]{1,0:T(4,128)}) custom-call(bf16[128,1536]{1,0:T(8,128)(2,1)} %q_ref.1, bf16[128,1536]{1,0:T(8,128)(2,1)} %k_ref.1, bf16[128,1536]{1,0:T(8,128)(2,1)} %v_hbm.1, f32[1536]{0:T(1024)} %qg_ref.1, f32[1536]{0:T(1024)} %kg_ref.1, f32[1,160]{1,0:T(1,128)} %bitcast.3, ...), custom_call_target="tpu_custom_call" | custom-call | tf_op jit(solution)/shard_map/pallas_call | solution.py:331
  69.7 4.1 %shard_map.114 = (bf16[128,2560]{1,0:T(8,128)(2,1)}, bf16[128,2560]{1,0:T(8,128)(2,1)}) custom-call(bf16[128,2560]{1,0:T(8,128)(2,1)} %get-tuple-element.5.hidden_ref, f32[2,128,128]{2,1,0:T(8,128)} %get-tuple-element.6.row_ref, f32[3,2560]{1,0:T(4,128)} %get-tuple-element.7.mod_ref), custom_call_target="tpu_custom_call" | custom-call | tf_op jit(solution)/shard_map/pallas_call | solution.py:373
